TPU v7x, 32 devices: a whole 2x2x4 slice. The times are simulated.
32 devices in a mesh: section: 8 (over z, x), dp: 4 (over y, core).
Axes of the slice: x: 2, y: 2, z: 4, core: 2. Of those that a mesh axis runs over, the one named last changes fastest.
Arguments:
- block_arguments: bfloat16 [2, 4, 1024, 2048], P(None, 'dp', 'section'), may hold values from -6 to 6
- incoming_batches: bfloat16 [2, 4, 128, 2048], P(None, 'dp'), may hold values from -6 to 6
- output_adjoints: bfloat16 [2, 4, 1024, 2048], P(None, 'dp', 'section'), may hold values from -0.125 to 0.125
- objective_adjoints: bfloat16 [2, 4, 128, 2048], P(None, 'dp'), may hold values from -0.125 to 0.125
- kept_block_arguments: bfloat16 [2, 2, 4, 1024, 2048], P(None, None, 'dp', 'section'), may hold values from -6 to 6
- parameter_arrays: bfloat16 [8, 2048, 1536], P('section', 'dp'), may hold values from -0.125 to 0.125
Outputs:
- ahead_out: bfloat16 [2, 4, 1024, 2048], P(None, 'dp', 'section')
- section_grads: float32 [8, 2048, 1536], P('section', 'dp')
All inputs are finite; a program needn't handle non-finite values.
Results may differ from a plain program's by a relative error of at most 0.013.
Values may be sent and summed in bfloat16 or wider, within the bound.
A program may use at most 128 MiB of HBM per device.

v0:
```python
import jax
import jax.numpy as jnp
from jax import lax
from jax.sharding import PartitionSpec as P


def mirrored(block, axis):
    count = lax.axis_size(axis)
    return lax.ppermute(block, axis, [(i, count - 1 - i) for i in range(count)])


def passed_along(block, axis, distance):
    devices = range(lax.axis_size(axis))
    route = [(i - distance, i) for i in devices if i - distance in devices]
    return lax.ppermute(block, axis, route)


def normalize(row_block):
    values = row_block.astype(jnp.float32)
    inverse = lax.rsqrt(jnp.mean(values * values, axis=-1, keepdims=True) + 1e-06)
    return (values, inverse, (values * inverse).astype(jnp.bfloat16))


def section_forward(row_block, matrix):
    hidden_width = matrix.shape[1] // 3
    values, inverse, normed = normalize(row_block)
    projected = jnp.dot(normed, matrix[:, : 2 * hidden_width], preferred_element_type=jnp.float32)
    gate_part = projected[:, :hidden_width]
    up_part = projected[:, hidden_width:]
    hidden = (gate_part * jax.nn.sigmoid(gate_part) * up_part).astype(jnp.bfloat16)
    branch = lax.dot_general(
        hidden,
        matrix[:, 2 * hidden_width :],
        (((1,), (1,)), ((), ())),
        preferred_element_type=jnp.float32,
    )
    return (values + branch).astype(jnp.bfloat16)


def reverse_parts(row_block, cotangent, matrix, with_input):
    hidden_width = matrix.shape[1] // 3
    values, inverse, normed = normalize(row_block)
    projected = jnp.dot(normed, matrix[:, : 2 * hidden_width], preferred_element_type=jnp.float32)
    gate_part = projected[:, :hidden_width]
    up_part = projected[:, hidden_width:]
    sigmoid_gate = jax.nn.sigmoid(gate_part)
    silu_gate = gate_part * sigmoid_gate
    hidden = (silu_gate * up_part).astype(jnp.bfloat16)
    hidden_grad = jnp.dot(
        cotangent, matrix[:, 2 * hidden_width :], preferred_element_type=jnp.float32
    )
    projected_grad = jnp.concatenate(
        [
            hidden_grad * up_part * sigmoid_gate * (1.0 + gate_part * (1.0 - sigmoid_gate)),
            hidden_grad * silu_gate,
        ],
        axis=1,
    ).astype(jnp.bfloat16)
    pieces = (normed, projected_grad, cotangent, hidden)
    if not with_input:
        return (pieces, None)
    normed_grad = lax.dot_general(
        projected_grad,
        matrix[:, : 2 * hidden_width],
        (((1,), (1,)), ((), ())),
        preferred_element_type=jnp.float32,
    )
    inner_sum = jnp.mean(normed_grad * values, axis=-1, keepdims=True)
    input_grad = (
        cotangent.astype(jnp.float32)
        + inverse * normed_grad
        - values * inverse * inverse * inverse * inner_sum
    )
    return (pieces, input_grad.astype(jnp.bfloat16))


def weight_pieces(piece_list):
    normed = jnp.concatenate([item[0] for item in piece_list], axis=0)
    projected_grad = jnp.concatenate([item[1] for item in piece_list], axis=0)
    cotangent = jnp.concatenate([item[2] for item in piece_list], axis=0)
    hidden = jnp.concatenate([item[3] for item in piece_list], axis=0)
    inward_grad = lax.dot_general(
        normed, projected_grad, (((0,), (0,)), ((), ())), preferred_element_type=jnp.float32
    )
    outward_grad = lax.dot_general(
        cotangent, hidden, (((0,), (0,)), ((), ())), preferred_element_type=jnp.float32
    )
    return (inward_grad, outward_grad)


def on_device(
    block_arguments,
    incoming_batches,
    output_adjoints,
    objective_adjoints,
    kept_block_arguments,
    parameter_arrays,
):
    position = lax.axis_index("section")
    segment_sequence_catalog = lax.axis_size("section")
    own_slice = parameter_arrays[0]
    resident_parameter_array = lax.all_gather(own_slice, "dp", axis=0, tiled=True)
    first_section = position == 0
    last_section = position == segment_sequence_catalog - 1
    up_input = mirrored(block_arguments[1, 0], "section")
    up_first_rows = mirrored(kept_block_arguments[1, 0, 0], "section")
    up_first_cot = mirrored(output_adjoints[1, 0], "section")
    up_second_rows = mirrored(kept_block_arguments[1, 1, 0], "section")
    down_ahead = section_forward(block_arguments[0, 0], resident_parameter_array)
    up_ahead = section_forward(up_input, resident_parameter_array)
    down_first_parts, down_backward_flow = reverse_parts(
        kept_block_arguments[0, 0, 0], output_adjoints[0, 0], resident_parameter_array, True
    )
    upward_first_parts, upward_backward_flow = reverse_parts(
        up_first_rows, up_first_cot, resident_parameter_array, True
    )
    arrivals = [passed_along(item, "section", 1) for item in (down_ahead, up_ahead)]
    returns = [
        passed_along(item, "section", -1) for item in (down_backward_flow, upward_backward_flow)
    ]
    down_next = jnp.where(first_section, incoming_batches[0, 0], arrivals[0])
    up_next = jnp.where(first_section, incoming_batches[1, 0], arrivals[1])
    descending_adjoint = jnp.where(last_section, objective_adjoints[0, 0], returns[0])
    ascending_adjoint = jnp.where(last_section, objective_adjoints[1, 0], returns[1])
    down_out = section_forward(down_next, resident_parameter_array)
    up_out = section_forward(up_next, resident_parameter_array)
    down_second_parts, discarded_value = reverse_parts(
        kept_block_arguments[0, 1, 0], descending_adjoint, resident_parameter_array, False
    )
    upward_second_parts, discarded_second = reverse_parts(
        up_second_rows, ascending_adjoint, resident_parameter_array, False
    )
    inward_grad, outward_grad = weight_pieces(
        [down_first_parts, down_second_parts, upward_first_parts, upward_second_parts]
    )
    inward_sum, outward_sum = (
        lax.psum_scatter(
            inward_grad.astype(jnp.bfloat16), "dp", scatter_dimension=0, tiled=True
        ).astype(jnp.float32),
        lax.psum_scatter(
            outward_grad.astype(jnp.bfloat16), "dp", scatter_dimension=0, tiled=True
        ).astype(jnp.float32),
    )
    up_out = mirrored(up_out, "section")
    ahead_out = jnp.stack([down_out, up_out])[:, None]
    return (ahead_out, jnp.concatenate([inward_sum, outward_sum], axis=1)[None])


def solution(mesh):
    in_specs = (
        P(None, "dp", "section", None),
        P(None, "dp", None, None),
        P(None, "dp", "section", None),
        P(None, "dp", None, None),
        P(None, None, "dp", "section", None),
        P("section", "dp", None),
    )
    out_specs = (P(None, "dp", "section", None), P("section", "dp", None))
    return jax.shard_map(
        on_device, mesh=mesh, in_specs=in_specs, out_specs=out_specs, check_vma=False
    )
```

profile of v0, /device:TPU:21, one launch (start us, length us, event | category | flops | bytes accessed | tf_op | source)
XLA Modules:
  0.0 226.4 jit_solution(2115386564319349945)
XLA Ops:
  7.2 0.7 all-gather.3.cloned.1.call-update
  8.0 2.3 %slice_bitcast_fusion.2 = (bf16[128,2048]{1,0:T(8,128)(2,1)}, bf16[128,2048]{1,0:T(8,128)(2,1)}) fusion(bf16[2,2,1,128,2048]{4,3,2,1,0:T(8,128)(2,1)} %param.10), kind=kLoop, calls=%fused_computation.107 | loop fusion | bytes 2097152 | tf_op jit(solution)/shard_map/squeeze | solution.py:108
  10.3 1.1 collective-permute-start.4
  11.4 2.3 %slice_bitcast_fusion.1 = (bf16[128,2048]{1,0:T(8,128)(2,1)}, bf16[128,2048]{1,0:T(8,128)(2,1)}) fusion(bf16[2,1,128,2048]{3,2,1,0:T(8,128)(2,1)} %param.8), kind=kLoop, calls=%fused_computation.106 | loop fusion | bytes 2097152 | tf_op jit(solution)/shard_map/squeeze | solution.py:112
  13.6 1.3 collective-permute-start.7
  14.9 1.1 collective-permute-start.5
  16.2 1.0 fusion.23
  17.2 40.7 %collective-permute-done.4 = bf16[128,2048]{1,0:T(8,128)(2,1)S(1)} collective-permute-done((bf16[128,2048]{1,0:T(8,128)(2,1)}, bf16[128,2048]{1,0:T(8,128)(2,1)S(1)}, u32[]{:S(2)}, u32[]{:S(2)}) %collective-permute-start.4) | collective-permute-done | bytes 524320 | tf_op jit(solution)/shard_map/ppermute | solution.py:9
  58.1 22.3 %collective-permute-done.5 = bf16[128,2048]{1,0:T(8,128)(2,1)S(1)} collective-permute-done((bf16[128,2048]{1,0:T(8,128)(2,1)}, bf16[128,2048]{1,0:T(8,128)(2,1)S(1)}, u32[]{:S(2)}, u32[]{:S(2)}) %collective-permute-start.5) | collective-permute-done | bytes 524320 | tf_op jit(solution)/shard_map/ppermute | solution.py:9
  80.6 1.0 fusion.21
  81.5 1.0 fusion.33
  82.5 3.2 %fusion.136 = f32[128,1024]{1,0:T(8,128)S(1)} fusion(bf16[128,2048]{1,0:T(8,128)(2,1)} %fusion.23, bf16[2048,1536]{1,0:T(8,128)(2,1)} %bitcast.64), kind=kOutput, calls=%fused_computation.193 | convolution fusion | flops 536870912 | bytes 5242880 | tf_op jit(solution)/shard_map/dot_general | solution.py:43
  85.7 2.4 %multiply_convert_fusion.11 = (bf16[128,512]{1,0:T(8,128)(2,1)S(1)}, bf16[128,512]{1,0:T(8,128)(2,1)S(1)}, bf16[128,512]{1,0:T(8,128)(2,1)S(1)}) fusion(f32[128,1024]{1,0:T(8,128)S(1)} %fusion.136, bf16[2048,1536]{1,0:T(8,128)(2,1)} %bitcast.65, bf16[2,1,128,2048]{3,2,1,0:T(8,128)(2,1)S(1)} %copy-done.1), kind=kOutput, calls=%fused_computation.160 | convolution fusion | flops 269418496 | bytes 3538944 | tf_op jit(solution)/shard_map/dot_general | solution.py:49
  88.2 1.6 fusion.34
  90.3 3.2 %collective-permute-start.6 = (bf16[128,2048]{1,0:T(8,128)(2,1)S(1)}, bf16[128,2048]{1,0:T(8,128)(2,1)S(1)}, u32[]{:S(2)}, u32[]{:S(2)}) collective-permute-start(bf16[128,2048]{1,0:T(8,128)(2,1)S(1)} %get-tuple-element.11), channel_id=1, source_target_pairs={{4,0},{8,4},{12,8},{16,12},{20,16},{24,20},{28,24},{5,1},{9,5},{13... | collective-permute-start | bytes 1572872 | tf_op jit(solution)/shard_map/ppermute | solution.py:15
  93.5 0.7 fusion.131
  94.3 1.6 multiply_convert_fusion.7
  95.9 1.6 fusion.43
  97.5 1.4 fusion.31
  98.9 2.1 collective-permute-start.8
  101.0 0.7 fusion.128
  101.8 0.7 fusion.133
  102.5 1.6 collective-permute-done.6
  104.1 11.2 %collective-permute-done.8 = bf16[128,2048]{1,0:T(8,128)(2,1)S(1)} collective-permute-done((bf16[128,2048]{1,0:T(8,128)(2,1)S(1)}, bf16[128,2048]{1,0:T(8,128)(2,1)S(1)}, u32[]{:S(2)}, u32[]{:S(2)}) %collective-permute-start.8) | collective-permute-done | bytes 524320 | tf_op jit(solution)/shard_map/ppermute | solution.py:15
  115.5 0.5 multiply_convert_fusion.5
  116.0 0.5 multiply_convert_fusion.9
  116.5 3.8 %convolution_convert_fusion.1 = bf16[2048,512]{1,0:T(8,128)(2,1)} fusion(bf16[128,2048]{1,0:T(8,128)(2,1)S(1)} %get-tuple-element.17, bf16[128,2048]{1,0:T(8,128)(2,1)} %collective-permute-done.7, bf16[128,2048]{1,0:T(8,128)(2,1)S(1)} %get-tuple-element.16, bf16[128,2048]{1,0:T(8,128)(2,1)S(1)} %copy-done.8, bf16[128,512]{1,0:T(8,128)(2,1)S(1)} %get-tuple-element.29, ...), kind=kOutput, calls=%fused_computation.1 | convolution fusion | flops 1085276160 | bytes 4718592 | tf_op jit(solution)/shard_map/dot_general | solution.py:85
  120.6 4.4 %convolution_convert_fusion = bf16[2048,1024]{1,0:T(8,128)(2,1)} fusion(bf16[128,2048]{1,0:T(8,128)(2,1)S(1)} %copy-done.7, bf16[128,2048]{1,0:T(8,128)(2,1)S(1)} %copy-done.6, bf16[128,2048]{1,0:T(8,128)(2,1)S(1)} %copy-done.10, bf16[128,2048]{1,0:T(8,128)(2,1)S(1)} %copy-done.5, bf16[128,512]{1,0:T(8,128)(2,1)S(1)} %get-tuple-element.23, ...), kind=kOutput, calls=%fused_computation | convolution fusion | flops 2166358016 | bytes 7340032 | tf_op jit(solution)/shard_map/dot_general | solution.py:82
  125.0 1.2 copy-done.3
  126.2 2.6 %collective-permute-start.1 = (bf16[128,2048]{1,0:T(8,128)(2,1)S(1)}, bf16[128,2048]{1,0:T(8,128)(2,1)S(1)}, u32[]{:S(2)}, u32[]{:S(2)}) collective-permute-start(bf16[128,2048]{1,0:T(8,128)(2,1)S(1)} %slice_bitcast_fusion.4), channel_id=1, source_target_pairs={{0,28},{4,24},{8,20},{12,16},{16,12},{20,8},{24,4},{28,0},{1,29},{... | collective-permute-start | bytes 1572872 | tf_op jit(solution)/shard_map/ppermute | solution.py:9
  129.0 22.8 %collective-permute-done.1 = bf16[128,2048]{1,0:T(8,128)(2,1)S(1)} collective-permute-done((bf16[128,2048]{1,0:T(8,128)(2,1)S(1)}, bf16[128,2048]{1,0:T(8,128)(2,1)S(1)}, u32[]{:S(2)}, u32[]{:S(2)}) %collective-permute-start.1) | collective-permute-done | bytes 524320 | tf_op jit(solution)/shard_map/ppermute | solution.py:9
  152.0 3.1 %fusion.63 = f32[128,1024]{1,0:T(8,128)S(1)} fusion(f32[128]{0:T(128)S(1)} %add_rsqrt_fusion.7, bf16[2,1,128,2048]{3,2,1,0:T(8,128)(2,1)S(1)} %copy-done.3, bf16[2048,1536]{1,0:T(8,128)(2,1)} %bitcast.66), kind=kOutput, calls=%fused_computation.89 | convolution fusion | flops 537657344 | bytes 5243392 | tf_op jit(solution)/shard_map/dot_general | solution.py:27
  155.1 2.4 %fusion = bf16[128,2048]{1,0:T(8,128)(2,1)S(1)} fusion(bf16[2,1,128,2048]{3,2,1,0:T(8,128)(2,1)S(1)} %copy-done.3, bf16[2048,1536]{1,0:T(8,128)(2,1)} %bitcast.67, f32[128,1024]{1,0:T(8,128)S(1)} %fusion.63), kind=kOutput, calls=%fused_computation.6 | convolution fusion | flops 269615104 | bytes 3670016 | tf_op jit(solution)/shard_map/dot_general | solution.py:31
  157.6 2.1 collective-permute-start
  159.6 0.8 fusion.67
  160.4 0.8 fusion.2
  161.2 1.9 collective-permute-start.2
  163.2 10.5 %collective-permute-done = bf16[128,2048]{1,0:T(8,128)(2,1)S(1)} collective-permute-done((bf16[128,2048]{1,0:T(8,128)(2,1)S(1)}, bf16[128,2048]{1,0:T(8,128)(2,1)S(1)}, u32[]{:S(2)}, u32[]{:S(2)}) %collective-permute-start) | collective-permute-done | bytes 524320 | tf_op jit(solution)/shard_map/ppermute | solution.py:15
  173.7 11.2 %collective-permute-done.2 = bf16[128,2048]{1,0:T(8,128)(2,1)S(1)} collective-permute-done((bf16[128,2048]{1,0:T(8,128)(2,1)S(1)}, bf16[128,2048]{1,0:T(8,128)(2,1)S(1)}, u32[]{:S(2)}, u32[]{:S(2)}) %collective-permute-start.2) | collective-permute-done | bytes 524320 | tf_op jit(solution)/shard_map/ppermute | solution.py:15
  184.9 0.5 fusion.36
  185.4 3.2 %fusion.65 = f32[128,1024]{1,0:T(8,128)S(1)} fusion(bf16[128,2048]{1,0:T(8,128)(2,1)S(1)} %get-tuple-element.19, f32[128]{0:T(128)S(1)} %add_rsqrt_fusion.4, bf16[2048,1536]{1,0:T(8,128)(2,1)} %bitcast.68), kind=kOutput, calls=%fused_computation.90 | convolution fusion | flops 537657344 | bytes 5243392 | tf_op jit(solution)/shard_map/dot_general | solution.py:27
  188.7 2.4 %fusion.3 = bf16[128,2048]{1,0:T(8,128)(2,1)S(1)} fusion(bf16[128,2048]{1,0:T(8,128)(2,1)S(1)} %get-tuple-element.19, bf16[2048,1536]{1,0:T(8,128)(2,1)} %bitcast.69, f32[128,1024]{1,0:T(8,128)S(1)} %fusion.65), kind=kOutput, calls=%fused_computation.9 | convolution fusion | flops 269615104 | bytes 3670016 | tf_op jit(solution)/shard_map/dot_general | solution.py:31
  191.1 1.8 collective-permute-start.3
  193.0 0.8 fusion.69
  193.8 0.8 fusion.4
  194.6 20.8 %collective-permute-done.3 = bf16[128,2048]{1,0:T(8,128)(2,1)S(1)} collective-permute-done((bf16[128,2048]{1,0:T(8,128)(2,1)S(1)}, bf16[128,2048]{1,0:T(8,128)(2,1)S(1)}, u32[]{:S(2)}, u32[]{:S(2)}) %collective-permute-start.3) | collective-permute-done | bytes 524320 | tf_op jit(solution)/shard_map/ppermute | solution.py:9
  215.4 1.1 maximum_bitcast_fusion.1
  216.5 3.4 %fusion.19 = f32[1,512,1536]{2,1,0:T(8,128)} fusion(bf16[512,512]{1,0:T(8,128)(2,1)} %reduce-scatter.5.cloned.1.call-done, bf16[512,1024]{1,0:T(8,128)(2,1)} %reduce-scatter.3.cloned.1.call-done), kind=kLoop, calls=%fused_computation.26 | loop fusion | flops 3932160 | bytes 4718592 | tf_op jit(solution)/shard_map/broadcast_in_dim | solution.py:146
  (59 shorter events, 2.0 us)
Async XLA Ops:
  7.2 8.8 %copy-start = (bf16[2,2,1,128,2048]{4,3,2,1,0:T(8,128)(2,1)S(1)}, bf16[2,2,1,128,2048]{4,3,2,1,0:T(8,128)(2,1)}, u32[]{:S(2)}) copy-start(bf16[2,2,1,128,2048]{4,3,2,1,0:T(8,128)(2,1)} %param.10) | copy-start | bytes 6291460
  7.2 75.3 %all-gather.3.cloned.1.call-start = ((), (), s32[]{:S(2)}) async-start(), calls=%async_computation.4 | async-start | bytes 7864320 | tf_op jit(solution)/shard_map/all_gather | solution.py:102
  7.9 208.5 %reduce-scatter.5.cloned.1.call-start = ((), (), s32[]{:S(2)}) async-start(), calls=%async_computation.3 | async-start | bytes 2621440 | tf_op jit(solution)/shard_map/reduce_scatter | solution.py:140
  10.3 47.6 %collective-permute-start.4 = (bf16[128,2048]{1,0:T(8,128)(2,1)}, bf16[128,2048]{1,0:T(8,128)(2,1)S(1)}, u32[]{:S(2)}, u32[]{:S(2)}) collective-permute-start(bf16[128,2048]{1,0:T(8,128)(2,1)} %get-tuple-element.13), channel_id=1, source_target_pairs={{0,28},{4,24},{8,20},{12,16},{16,12},{20,8},{24,4},{28,0},{1,29},{... | collective-permute-start | bytes 1572872 | tf_op jit(solution)/shard_map/ppermute | solution.py:9
  13.6 80.7 %collective-permute-start.7 = (bf16[128,2048]{1,0:T(8,128)(2,1)}, bf16[128,2048]{1,0:T(8,128)(2,1)}, u32[]{:S(2)}, u32[]{:S(2)}) collective-permute-start(bf16[128,2048]{1,0:T(8,128)(2,1)} %get-tuple-element.15), channel_id=1, source_target_pairs={{0,28},{4,24},{8,20},{12,16},{16,12},{20,8},{24,4},{28,0},{1,29},{... | collective-permute-start | bytes 1572872 | tf_op jit(solution)/shard_map/ppermute | solution.py:9
  14.9 65.5 %collective-permute-start.5 = (bf16[128,2048]{1,0:T(8,128)(2,1)}, bf16[128,2048]{1,0:T(8,128)(2,1)S(1)}, u32[]{:S(2)}, u32[]{:S(2)}) collective-permute-start(bf16[128,2048]{1,0:T(8,128)(2,1)} %get-tuple-element.12), channel_id=1, source_target_pairs={{0,28},{4,24},{8,20},{12,16},{16,12},{20,8},{24,4},{28,0},{1,29},{... | collective-permute-start | bytes 1572872 | tf_op jit(solution)/shard_map/ppermute | solution.py:9
  82.5 3.2 %copy-start.1 = (bf16[2,1,128,2048]{3,2,1,0:T(8,128)(2,1)S(1)}, bf16[2,1,128,2048]{3,2,1,0:T(8,128)(2,1)}, u32[]{:S(2)}) copy-start(bf16[2,1,128,2048]{3,2,1,0:T(8,128)(2,1)} %param.8) | copy-start | bytes 3145732
  82.5 5.7 %copy-start.11 = (bf16[1,2048,1536]{2,1,0:T(8,128)(2,1)S(1)}, bf16[1,2048,1536]{2,1,0:T(8,128)(2,1)}, u32[]{:S(2)}) copy-start(bf16[1,2048,1536]{2,1,0:T(8,128)(2,1)} %all-gather.3.cloned.1.call-done) | copy-start | bytes 18874372
  88.2 5.4 %copy-start.6 = (bf16[128,2048]{1,0:T(8,128)(2,1)S(1)}, bf16[128,2048]{1,0:T(8,128)(2,1)}, u32[]{:S(2)}) copy-start(bf16[128,2048]{1,0:T(8,128)(2,1)} %fusion.21) | copy-start | bytes 1572868
  90.3 11.5 %copy-start.9 = (bf16[128,2048]{1,0:T(8,128)(2,1)}, bf16[128,2048]{1,0:T(8,128)(2,1)S(1)}, u32[]{:S(2)}) copy-start(bf16[128,2048]{1,0:T(8,128)(2,1)S(1)} %get-tuple-element.10) | copy-start | bytes 1572868
  90.3 13.8 %collective-permute-start.6 = (bf16[128,2048]{1,0:T(8,128)(2,1)S(1)}, bf16[128,2048]{1,0:T(8,128)(2,1)S(1)}, u32[]{:S(2)}, u32[]{:S(2)}) collective-permute-start(bf16[128,2048]{1,0:T(8,128)(2,1)S(1)} %get-tuple-element.11), channel_id=1, source_target_pairs={{4,0},{8,4},{12,8},{16,12},{20,16},{24,20},{28,24},{5,1},{9,5},{13... | collective-permute-start | bytes 1572872 | tf_op jit(solution)/shard_map/ppermute | solution.py:15
  95.9 5.1 %copy-start.7 = (bf16[128,2048]{1,0:T(8,128)(2,1)S(1)}, bf16[128,2048]{1,0:T(8,128)(2,1)}, u32[]{:S(2)}) copy-start(bf16[128,2048]{1,0:T(8,128)(2,1)} %fusion.33) | copy-start | bytes 1572868
  98.9 16.4 %collective-permute-start.8 = (bf16[128,2048]{1,0:T(8,128)(2,1)S(1)}, bf16[128,2048]{1,0:T(8,128)(2,1)S(1)}, u32[]{:S(2)}, u32[]{:S(2)}) collective-permute-start(bf16[128,2048]{1,0:T(8,128)(2,1)S(1)} %fusion.31), channel_id=1, source_target_pairs={{4,0},{8,4},{12,8},{16,12},{20,16},{24,20},{28,24},{5,1},{9,5},{13... | collective-permute-start | bytes 1572872 | tf_op jit(solution)/shard_map/ppermute | solution.py:15
  101.8 13.6 %copy-start.2 = (bf16[2,1,128,2048]{3,2,1,0:T(8,128)(2,1)S(1)}, bf16[2,1,128,2048]{3,2,1,0:T(8,128)(2,1)}, u32[]{:S(2)}) copy-start(bf16[2,1,128,2048]{3,2,1,0:T(8,128)(2,1)} %param.9) | copy-start | bytes 3145732
  115.5 1.0 copy-start.8
  116.5 4.0 %copy-start.5 = (bf16[128,2048]{1,0:T(8,128)(2,1)S(1)}, bf16[128,2048]{1,0:T(8,128)(2,1)}, u32[]{:S(2)}) copy-start(bf16[128,2048]{1,0:T(8,128)(2,1)} %fusion.23) | copy-start | bytes 1572868
  116.5 4.0 %copy-start.10 = (bf16[128,2048]{1,0:T(8,128)(2,1)S(1)}, bf16[128,2048]{1,0:T(8,128)(2,1)}, u32[]{:S(2)}) copy-start(bf16[128,2048]{1,0:T(8,128)(2,1)} %copy-done.9) | copy-start | bytes 1572868
  120.3 96.1 %reduce-scatter.3.cloned.1.call-start = ((), (), s32[]{:S(2)}) async-start(), calls=%async_computation.2 | async-start | bytes 5242880 | tf_op jit(solution)/shard_map/reduce_scatter | solution.py:137
  125.0 1.2 copy-start.3
  126.2 25.5 %collective-permute-start.1 = (bf16[128,2048]{1,0:T(8,128)(2,1)S(1)}, bf16[128,2048]{1,0:T(8,128)(2,1)S(1)}, u32[]{:S(2)}, u32[]{:S(2)}) collective-permute-start(bf16[128,2048]{1,0:T(8,128)(2,1)S(1)} %slice_bitcast_fusion.4), channel_id=1, source_target_pairs={{0,28},{4,24},{8,20},{12,16},{16,12},{20,8},{24,4},{28,0},{1,29},{... | collective-permute-start | bytes 1572872 | tf_op jit(solution)/shard_map/ppermute | solution.py:9
  152.0 7.7 %slice-start = ((s8[6291456]{0:T(1024)(128)(4,1)}), s8[4194304]{0:T(1024)(128)(4,1)S(1)}, s32[]{:S(2)}) async-start(s8[6291456]{0:T(1024)(128)(4,1)} %bitcast.78), calls=%async_computation.5 | async-start | bytes 8388608
  152.0 7.7 %slice-start.1 = ((s8[6291456]{0:T(1024)(128)(4,1)}), s8[2097152]{0:T(1024)(128)(4,1)S(1)}, s32[]{:S(2)}) async-start(s8[6291456]{0:T(1024)(128)(4,1)} %bitcast.78), calls=%async_computation.6 | async-start | bytes 4194304
  157.5 27.4 %copy-start.4 = (bf16[2,1,128,2048]{3,2,1,0:T(8,128)(2,1)S(1)}, bf16[2,1,128,2048]{3,2,1,0:T(8,128)(2,1)}, u32[]{:S(2)}) copy-start(bf16[2,1,128,2048]{3,2,1,0:T(8,128)(2,1)} %param.7) | copy-start | bytes 3145732
  157.6 16.1 %collective-permute-start = (bf16[128,2048]{1,0:T(8,128)(2,1)S(1)}, bf16[128,2048]{1,0:T(8,128)(2,1)S(1)}, u32[]{:S(2)}, u32[]{:S(2)}) collective-permute-start(bf16[128,2048]{1,0:T(8,128)(2,1)S(1)} %fusion), channel_id=1, source_target_pairs={{0,4},{4,8},{8,12},{12,16},{16,20},{20,24},{24,28},{1,5},{5,9},{9,... | collective-permute-start | bytes 1572872 | tf_op jit(solution)/shard_map/ppermute | solution.py:15
  161.2 23.7 %collective-permute-start.2 = (bf16[128,2048]{1,0:T(8,128)(2,1)S(1)}, bf16[128,2048]{1,0:T(8,128)(2,1)S(1)}, u32[]{:S(2)}, u32[]{:S(2)}) collective-permute-start(bf16[128,2048]{1,0:T(8,128)(2,1)S(1)} %fusion.2), channel_id=1, source_target_pairs={{0,4},{4,8},{8,12},{12,16},{16,20},{20,24},{24,28},{1,5},{5,9},{9,... | collective-permute-start | bytes 1572872 | tf_op jit(solution)/shard_map/ppermute | solution.py:15
  184.9 8.0 %slice-start.2 = ((s8[6291456]{0:T(1024)(128)(4,1)}), s8[4194304]{0:T(1024)(128)(4,1)S(1)}, s32[]{:S(2)}) async-start(s8[6291456]{0:T(1024)(128)(4,1)} %bitcast.82), calls=%async_computation.7 | async-start | bytes 8388608
  185.4 7.5 %slice-start.3 = ((s8[6291456]{0:T(1024)(128)(4,1)}), s8[2097152]{0:T(1024)(128)(4,1)S(1)}, s32[]{:S(2)}) async-start(s8[6291456]{0:T(1024)(128)(4,1)} %bitcast.82), calls=%async_computation.8 | async-start | bytes 4194304
  191.1 24.3 %collective-permute-start.3 = (bf16[128,2048]{1,0:T(8,128)(2,1)S(1)}, bf16[128,2048]{1,0:T(8,128)(2,1)S(1)}, u32[]{:S(2)}, u32[]{:S(2)}) collective-permute-start(bf16[128,2048]{1,0:T(8,128)(2,1)S(1)} %fusion.3), channel_id=1, source_target_pairs={{0,28},{4,24},{8,20},{12,16},{16,12},{20,8},{24,4},{28,0},{1,29},{... | collective-permute-start | bytes 1572872 | tf_op jit(solution)/shard_map/ppermute | solution.py:9
Sparse Core Ops, SparseCore 0:
  9.5 46.9 all-gather.2
  120.4 32.6 reduce-scatter.4
  155.7 44.5 reduce-scatter.2
where the time goes:
time: 227 us; the launch traced here: 226 us
  waiting for transfers between devices  142 us (63%)
  matrix products  36.1 us (16%)
  starting transfers between devices  17.4 us (8%)
  between operations  14.2 us (6%)
  other arithmetic  10.9 us (5%)
  local copies, waits for them, and re-layouts  5.9 us (3%)
    ppermute x5, waiting for transfers between devices, mirrored(): return lax.ppermute(block, axis, [(i, count - 1 - i) for i in range(count)])  107 us
    ppermute x4, waiting for transfers between devices, passed_along(): return lax.ppermute(block, axis, route)  34.6 us
    ppermute x4, starting transfers between devices, passed_along(): return lax.ppermute(block, axis, route)  9.29 us
    dot_general x4, matrix products, section_forward(): jnp.dot(normed, matrix[:, :2 * hidden_width], preferred_element_type=jnp....  7.9 us
    ppermute x5, starting transfers between devices, mirrored(): return lax.ppermute(block, axis, [(i, count - 1 - i) for i in range(count)])  7.85 us
    dot_general x4, matrix products, section_forward(): lax.dot_general(hidden, matrix[:, 2 * hidden_width:], (((1,), (1,)), ((),...  6.5 us
    dot_general x4, matrix products, reverse_parts(): jnp.dot(normed, matrix[:, :2 * hidden_width], preferred_element_type=jnp....  5.4 us
    dot_general x4, matrix products, reverse_parts(): jnp.dot(cotangent, matrix[:, 2 * hidden_width:], preferred_element_type=j...  4.99 us
  transfers between devices with their start and end apart: 12, of which 8 were waited for; matrix products, arithmetic and copies ran while one was open for 19% of the time, Pallas kernels for 0%

commit v1 on v0

v1 whole, which is shorter than its diff:
```python
import functools

import jax
import jax.numpy as jnp
from jax import lax
from jax.experimental import pallas as pl
from jax.experimental.pallas import tpu as pltpu
from jax.sharding import PartitionSpec as P

MESH = pl.DeviceIdType.MESH
BF = jnp.bfloat16
F32 = jnp.float32
TILE = 256
CHUNK = 128
NT = (((1,), (1,)), ((), ()))
TN = (((0,), (0,)), ((), ()))


def normalize_into(src, dst):
    values = src[...].astype(F32)
    inverse = lax.rsqrt(jnp.mean(values * values, axis=-1, keepdims=True) + 1e-06)
    dst[...] = (values * inverse).astype(BF)
    return inverse


def tiles(count, body):
    def step(j, carry):
        body(pl.multiple_of(j * TILE, TILE))
        return carry

    lax.fori_loop(0, count // TILE, step, 0)


def forward(rows, out, weights, normed, hidden):
    width = weights.shape[1] // 3
    normalize_into(rows, normed)

    def hidden_tile(at):
        gate = jnp.dot(normed[...], weights[:, pl.ds(at, TILE)], preferred_element_type=F32)
        up = jnp.dot(normed[...], weights[:, pl.ds(width + at, TILE)], preferred_element_type=F32)
        hidden[:, pl.ds(at, TILE)] = (gate * jax.nn.sigmoid(gate) * up).astype(BF)

    tiles(width, hidden_tile)

    def out_tile(at):
        branch = lax.dot_general(
            hidden[...], weights[pl.ds(at, TILE), 2 * width :], NT, preferred_element_type=F32
        )
        out[:, pl.ds(at, TILE)] = (rows[:, pl.ds(at, TILE)].astype(F32) + branch).astype(BF)

    tiles(weights.shape[0], out_tile)


def backward(rows, cotangent, weights, normed, hidden, pre_grad, back, scratch):
    width = weights.shape[1] // 3
    inverse = normalize_into(rows, normed)

    def hidden_tile(at):
        gate = jnp.dot(normed[...], weights[:, pl.ds(at, TILE)], preferred_element_type=F32)
        up = jnp.dot(normed[...], weights[:, pl.ds(width + at, TILE)], preferred_element_type=F32)
        grad = jnp.dot(
            cotangent[...], weights[:, pl.ds(2 * width + at, TILE)], preferred_element_type=F32
        )
        sig = jax.nn.sigmoid(gate)
        silu = gate * sig
        hidden[:, pl.ds(at, TILE)] = (silu * up).astype(BF)
        pre_grad[:, pl.ds(at, TILE)] = (grad * up * sig * (1.0 + gate * (1.0 - sig))).astype(BF)
        pre_grad[:, pl.ds(width + at, TILE)] = (grad * silu).astype(BF)

    tiles(width, hidden_tile)
    if back is None:
        return

    def grad_tile(at):
        scratch[:, pl.ds(at, TILE)] = lax.dot_general(
            pre_grad[...], weights[pl.ds(at, TILE), : 2 * width], NT, preferred_element_type=F32
        )

    tiles(weights.shape[0], grad_tile)
    values = rows[...].astype(F32)
    grad = scratch[...]
    inner = jnp.mean(grad * values, axis=-1, keepdims=True)
    back[...] = (
        cotangent[...].astype(F32)
        + inverse * grad
        - values * (inverse * inverse * inverse * inner)
    ).astype(BF)


def kernel(
    sections, replicas,
    x_hbm, inc_hbm, cot_hbm, obj_hbm, kept_hbm, w_hbm,
    out_hbm, grads_hbm,
    weights, x1, x2, kept, cots, normed, pre_grad, hidden, fo, fb, out2,
    fwd_normed, fwd_hidden, scratch,
    part_send, part_recv, keep, sum_send, sum_recv, total,
    lsem, wsem_s, wsem_r, psem_s, psem_r, msem_s, msem_r, rsem_s, rsem_r, gsem_s, gsem_r, ysem_s, ysem_r,
):
    s = lax.axis_index("section")
    d = lax.axis_index("dp")
    span = x1.shape[0] // 2
    shard = w_hbm.shape[1]
    groups = replicas // 2
    g, c = d // 2, lax.rem(d, 2)
    partner = (s, g * 2 + 1 - c)
    mirror = (sections - 1 - s, d)
    not_first = s > 0
    not_last = s < sections - 1
    peers = [(s, lax.rem(g + t, groups) * 2 + c) for t in range(1, groups)]
    senders = [lax.rem(g - t + groups, groups) for t in range(1, groups)]

    def remote(src, dst, ss, rs, to):
        return pltpu.make_async_remote_copy(
            src_ref=src, dst_ref=dst, send_sem=ss, recv_sem=rs, device_id=to, device_id_type=MESH
        )

    low, high = pl.ds(0, span), pl.ds(span, span)
    half = [pl.ds(i * span, span) for i in range(4)]

    local = [
        (w_hbm.at[0], weights.at[pl.ds(pl.multiple_of(d * shard, shard), shard)]),
        (cot_hbm.at[0, 0], cots.at[half[0]]),
        (kept_hbm.at[0, 0, 0], kept.at[half[0]]),
        (x_hbm.at[0, 0], x1.at[low]),
        (kept_hbm.at[0, 1, 0], kept.at[half[2]]),
    ]
    local = [pltpu.make_async_copy(a, b, lsem.at[i]) for i, (a, b) in enumerate(local)]
    for copy in local:
        copy.start()
    edge_in = [pltpu.make_async_copy(inc_hbm.at[i, 0], x2.at[half[i]], lsem.at[5 + i]) for i in range(2)]
    edge_cot = [
        pltpu.make_async_copy(obj_hbm.at[i, 0], cots.at[half[2 + i]], lsem.at[7 + i]) for i in range(2)
    ]

    @pl.when(s == 0)
    def _():
        for copy in edge_in:
            copy.start()

    @pl.when(s == sections - 1)
    def _():
        for copy in edge_cot:
            copy.start()

    following = (lax.rem(s + 1, sections), d)
    preceding = (lax.rem(s + sections - 1, sections), d)
    greeted = [mirror, partner, following, preceding] + peers
    barrier = pltpu.get_barrier_semaphore()
    for to in greeted:
        pl.semaphore_signal(barrier, inc=1, device_id=to, device_id_type=MESH)
    pl.semaphore_wait(barrier, len(greeted))

    pieces = 2
    piece = shard // pieces

    def w_rows(owner, h):
        return weights.at[pl.ds(pl.multiple_of(owner * shard + h * piece, piece), piece)]

    w_out = [
        [remote(w_hbm.at[0, pl.ds(h * piece, piece)], w_rows(d, h), wsem_s.at[t, h], wsem_r.at[t, h], to) for h in range(pieces)]
        for t, to in enumerate(peers)
    ]
    for h in range(pieces):
        for row in w_out:
            row[h].start()

    def mirrored(src, dst, i):
        return remote(src, dst, msem_s.at[i], msem_r.at[i], mirror)

    m_cot = mirrored(cot_hbm.at[1, 0], cots.at[half[1]], 0)
    m_kept = mirrored(kept_hbm.at[1, 0, 0], kept.at[half[1]], 1)
    m_x = mirrored(x_hbm.at[1, 0], x1.at[high], 2)
    m_kept2 = mirrored(kept_hbm.at[1, 1, 0], kept.at[half[3]], 3)
    m_out = mirrored(out2.at[high], out_hbm.at[1, 0], 4)
    m_cot.start()
    m_kept.start()
    m_x.start()

    p_own = [remote(w_hbm.at[0, pl.ds(h * piece, piece)], w_rows(d, h), psem_s.at[0, h], psem_r.at[0, h], partner) for h in range(pieces)]
    for copy in p_own:
        copy.start()
    p_fwd = [
        [
            remote(w_rows(from_g * 2 + c, h), w_rows(from_g * 2 + c, h), psem_s.at[1 + t, h], psem_r.at[1 + t, h], partner)
            for h in range(pieces)
        ]
        for t, from_g in enumerate(senders)
    ]
    for h in range(pieces):
        for t in range(len(peers)):
            w_out[t][h].wait_recv()
            p_fwd[t][h].start()
    local[0].wait()
    for copies in [p_own] + p_fwd:
        for copy in copies:
            copy.wait_recv()

    relay_f = [remote(fo.at[half[i]], x2.at[half[i]], rsem_s.at[i], rsem_r.at[i], following) for i in range(2)]
    relay_b = [remote(fb.at[half[i]], cots.at[half[2 + i]], rsem_s.at[2 + i], rsem_r.at[2 + i], preceding) for i in range(2)]

    def back_first(i):
        r = half[i]
        backward(kept.at[r], cots.at[r], weights, normed.at[r], hidden.at[r], pre_grad.at[r], fb.at[r], scratch)

        @pl.when(not_first)
        def _():
            relay_b[i].start()

    def ahead_first(i):
        r = half[i]
        forward(x1.at[r], fo.at[r], weights, fwd_normed, fwd_hidden)

        @pl.when(not_last)
        def _():
            relay_f[i].start()

    def back_second(i):
        @pl.when(not_last)
        def _():
            relay_b[i].wait_recv()

        @pl.when(s == sections - 1)
        def _():
            edge_cot[i].wait()

        r = half[2 + i]
        backward(kept.at[r], cots.at[r], weights, normed.at[r], hidden.at[r], pre_grad.at[r], None, None)

    def ahead_second(i):
        @pl.when(not_first)
        def _():
            relay_f[i].wait_recv()

        @pl.when(s == 0)
        def _():
            edge_in[i].wait()

        forward(x2.at[half[i]], out2.at[half[i]], weights, fwd_normed, fwd_hidden)

    local[1].wait()
    local[2].wait()
    back_first(0)
    local[3].wait()
    ahead_first(0)
    m_cot.wait_recv()
    m_kept.wait_recv()
    back_first(1)
    m_kept2.start()
    m_x.wait_recv()
    ahead_first(1)
    local[4].wait()
    back_second(0)
    ahead_second(0)
    out_own = pltpu.make_async_copy(out2.at[low], out_hbm.at[0, 0], lsem.at[9])
    out_own.start()
    ahead_second(1)
    m_out.start()
    m_kept2.wait_recv()
    back_second(1)

    width = weights.shape[1] // 3
    per = shard // CHUNK

    def term(owner, q, put):
        at = pl.multiple_of(owner * shard + q * CHUNK, CHUNK)
        put(slice(0, 2 * width), lax.dot_general(normed[:, pl.ds(at, CHUNK)], pre_grad[...], TN, preferred_element_type=F32))
        put(slice(2 * width, 3 * width), lax.dot_general(cots[:, pl.ds(at, CHUNK)], hidden[...], TN, preferred_element_type=F32))

    def pair_copy(i):
        return remote(part_send.at[i], part_recv.at[i], gsem_s.at[i], gsem_r.at[i], partner)

    def give(owner_group, i, q):
        def put(columns, value):
            part_send[i, :, columns] = value.astype(BF)

        term(owner_group * 2 + 1 - c, q, put)
        pair_copy(i).start()

    def own_term(owner_group, q, store):
        term(owner_group * 2 + c, q, store)

    def loop(count, body):
        def step(q, carry):
            body(q)
            return carry

        lax.fori_loop(0, count, step, 0)

    def sum_copy(i, to):
        return remote(sum_send.at[i], sum_recv.at[i], ysem_s.at[i], ysem_r.at[i], to)

    for t in range(1, groups):
        to_g = lax.rem(g + t, groups)
        loop(per, lambda q: give(to_g, t * per + q, q))

        def pass_on(q):
            def put(columns, value):
                keep[:, columns] = value

            own_term(to_g, q, put)
            pair_copy(t * per + q).wait_recv()
            i = (t - 1) * per + q
            sum_send[i] = (keep[...] + part_recv[t * per + q].astype(F32)).astype(BF)
            sum_copy(i, peers[t - 1]).start()

        loop(per, pass_on)
    loop(per, lambda q: give(g, q, q))

    def finish(q):
        rows = pl.ds(pl.multiple_of(q * CHUNK, CHUNK), CHUNK)

        def put(columns, value):
            total[rows, columns] = value

        own_term(g, q, put)
        pair_copy(q).wait_recv()
        total[rows] = total[rows] + part_recv[q].astype(F32)

    loop(per, finish)

    def collect(q):
        rows = pl.ds(pl.multiple_of(q * CHUNK, CHUNK), CHUNK)
        value = total[rows]
        for t in range(1, groups):
            i = (t - 1) * per + q
            sum_copy(i, peers[t - 1]).wait_recv()
            value = value + sum_recv[i].astype(F32)
        total[rows] = value
        pltpu.make_async_copy(total.at[rows], grads_hbm.at[0, rows], lsem.at[10]).start()

    loop(per, collect)
    pltpu.make_async_copy(total, grads_hbm.at[0], lsem.at[10]).wait()

    out_own.wait()
    m_out.wait_recv()
    for copy in (m_cot, m_kept, m_x, m_kept2, m_out):
        copy.wait_send()
    for row in w_out + [p_own] + p_fwd:
        for copy in row:
            copy.wait_send()

    @pl.when(not_last)
    def _():
        for copy in relay_f:
            copy.wait_send()

    @pl.when(not_first)
    def _():
        for copy in relay_b:
            copy.wait_send()

    loop(groups * per, lambda i: pair_copy(i).wait_send())
    loop((groups - 1) * per, lambda i: sum_copy(i, peers[0]).wait_send())


def on_device(sections, replicas, x, inc, cot, obj, kept, w):
    span, features = x.shape[2:]
    shard, columns = w.shape[1:]
    width = columns // 3
    groups = replicas // 2
    pairs = groups * (shard // CHUNK)
    sums = max(1, (groups - 1) * (shard // CHUNK))
    dma = pltpu.SemaphoreType.DMA
    v = pltpu.VMEM
    any_space = pl.BlockSpec(memory_space=pl.ANY)
    return pl.pallas_call(
        functools.partial(kernel, sections, replicas),
        out_shape=(
            jax.ShapeDtypeStruct(x.shape, BF),
            jax.ShapeDtypeStruct(w.shape, F32),
        ),
        in_specs=[any_space] * 6,
        out_specs=(any_space, any_space),
        scratch_shapes=[
            v((features, columns), BF),
            v((2 * span, features), BF),
            v((2 * span, features), BF),
            v((4 * span, features), BF),
            v((4 * span, features), BF),
            v((4 * span, features), BF),
            v((4 * span, 2 * width), BF),
            v((4 * span, width), BF),
            v((2 * span, features), BF),
            v((2 * span, features), BF),
            v((2 * span, features), BF),
            v((span, features), BF),
            v((span, width), BF),
            v((span, features), F32),
            v((pairs, CHUNK, columns), BF),
            v((pairs, CHUNK, columns), BF),
            v((CHUNK, columns), F32),
            v((sums, CHUNK, columns), BF),
            v((sums, CHUNK, columns), BF),
            v((shard, columns), F32),
            dma((11,)),
            dma((groups, 2)),
            dma((groups, 2)),
            dma((groups, 2)),
            dma((groups, 2)),
            dma((5,)),
            dma((5,)),
            dma((4,)),
            dma((4,)),
            dma((pairs,)),
            dma((pairs,)),
            dma((sums,)),
            dma((sums,)),
        ],
        compiler_params=pltpu.CompilerParams(
            collective_id=0, has_side_effects=True, vmem_limit_bytes=60 * 2**20
        ),
    )(x, inc, cot, obj, kept, w)


def solution(mesh):
    in_specs = (
        P(None, "dp", "section", None),
        P(None, "dp", None, None),
        P(None, "dp", "section", None),
        P(None, "dp", None, None),
        P(None, None, "dp", "section", None),
        P("section", "dp", None),
    )
    out_specs = (P(None, "dp", "section", None), P("section", "dp", None))
    body = functools.partial(on_device, mesh.shape["section"], mesh.shape["dp"])
    return jax.shard_map(body, mesh=mesh, in_specs=in_specs, out_specs=out_specs, check_vma=False)
```

time: 227 us -> 190 us (0.84)
  the two profiles are of different devices: /device:TPU:21 before, /device:TPU:18 now
where the time goes in v1:
time: 190 us; the launch traced here: 189 us
  Pallas kernels  183 us (96%)
  local copies, waits for them, and re-layouts  6.06 us (3%)
    pallas_call x1, Pallas kernels, on_device(): pl.pallas_call(functools.partial(kernel, sections, replicas), out_shape=(...  183 us
    unnamed x2, local copies, waits for them, and re-layouts  6.06 us

profile of v1, /device:TPU:18, one launch (start us, length us, event | category | flops | bytes accessed | tf_op | source)
XLA Modules:
  0.0 189.5 jit_solution(2486857561932720233)
XLA Ops:
  0.6 182.8 %shard_map.77 = (bf16[2,1,128,2048]{3,2,1,0:T(8,128)(2,1)}, f32[1,512,1536]{2,1,0:T(8,128)}) custom-call(bf16[2,1,128,2048]{3,2,1,0:T(8,128)(2,1)} %x_hbm.1, bf16[2,1,128,2048]{3,2,1,0:T(8,128)(2,1)} %inc_hbm.1, bf16[2,1,128,2048]{3,2,1,0:T(8,128)(2,1)} %cot_hbm.1, bf16[2,1,128,2048]{3,2,1,0:T(8,128)(2,1)} %obj_hbm.1, ...), custom_call_target="tpu_custom_call" | custom-call | tf_op jit(solution)/shard_map/pallas_call | solution.py:366
  183.4 2.3 %copy.10 = bf16[2,1,128,2048]{3,2,1,0:T(8,128)(2,1)} copy(bf16[2,1,128,2048]{3,2,1,0:T(8,128)(2,1)} %get-tuple-element.4) | data formatting | bytes 2097152
  185.7 3.8 %copy.11 = f32[1,512,1536]{2,1,0:T(8,128)} copy(f32[1,512,1536]{2,1,0:T(8,128)} %get-tuple-element.5) | data formatting | bytes 6291456

commit v2 on v1

--- a/solution.py
+++ b/solution.py
@@ -92,9 +92,9 @@
     x_hbm, inc_hbm, cot_hbm, obj_hbm, kept_hbm, w_hbm,
     out_hbm, grads_hbm,
     weights, x1, x2, kept, cots, normed, pre_grad, hidden, fo, fb, out2,
-    fwd_normed, fwd_hidden, scratch,
+    fwd_normed, fwd_hidden, scratch, via_kept, via_x,
     part_send, part_recv, keep, sum_send, sum_recv, total,
-    lsem, wsem_s, wsem_r, psem_s, psem_r, msem_s, msem_r, rsem_s, rsem_r, gsem_s, gsem_r, ysem_s, ysem_r,
+    lsem, wsem_s, wsem_r, psem_s, psem_r, msem_s, msem_r, rsem_s, rsem_r, gsem_s, gsem_r, ysem_s, ysem_r, vsem_s, vsem_r, turn,
 ):
     s = lax.axis_index("section")
     d = lax.axis_index("dp")
@@ -144,7 +144,17 @@
 
     following = (lax.rem(s + 1, sections), d)
     preceding = (lax.rem(s + sections - 1, sections), d)
+    staged = sections == 8
     greeted = [mirror, partner, following, preceding] + peers
+    if staged:
+        above = s + 2 - 4 * lax.rem(s // 2, 2)
+        beside = s + 1 - 2 * lax.rem(s, 2)
+        outer = (s < 2) | (s >= sections - 2)
+        inner = (s >= 2) & (s < sections - 2)
+        middle = (s == sections // 2 - 1) | (s == sections // 2)
+        helper = (s == sections // 2 - 2) | (s == sections // 2 + 1)
+        direct = (s < sections // 2 - 1) | (s > sections // 2)
+        greeted += [(above, d), (sections - 1 - above, d), (sections - 1 - beside, d)]
     barrier = pltpu.get_barrier_semaphore()
     for to in greeted:
         pl.semaphore_signal(barrier, inc=1, device_id=to, device_id_type=MESH)
@@ -174,7 +184,19 @@
     m_out = mirrored(out2.at[high], out_hbm.at[1, 0], 4)
     m_cot.start()
     m_kept.start()
-    m_x.start()
+    if staged:
+        k_via = remote(kept_hbm.at[1, 1, 0], via_kept, vsem_s.at[0], vsem_r.at[0], (beside, d))
+        x_via = remote(x_hbm.at[1, 0], via_x, vsem_s.at[1], vsem_r.at[1], (above, d))
+        k_pass = remote(via_kept, kept.at[half[3]], vsem_s.at[2], msem_r.at[3], (sections - 1 - beside, d))
+        x_pass = remote(via_x, x1.at[high], vsem_s.at[3], msem_r.at[2], (sections - 1 - above, d))
+
+        @pl.when(middle)
+        def _():
+            k_via.start()
+
+        @pl.when(outer & not_first)
+        def _():
+            x_via.start()
 
     p_own = [remote(w_hbm.at[0, pl.ds(h * piece, piece)], w_rows(d, h), psem_s.at[0, h], psem_r.at[0, h], partner) for h in range(pieces)]
     for copy in p_own:
@@ -206,12 +228,13 @@
         def _():
             relay_b[i].start()
 
-    def ahead_first(i):
-        r = half[i]
-        forward(x1.at[r], fo.at[r], weights, fwd_normed, fwd_hidden)
-
-        @pl.when(not_last)
-        def _():
+    def ahead_first(i, here):
+        @pl.when(here & not_last)
+        def _():
+            if i:
+                m_x.wait_recv()
+            r = half[i]
+            forward(x1.at[r], fo.at[r], weights, fwd_normed, fwd_hidden)
             relay_f[i].start()
 
     def back_second(i):
@@ -227,34 +250,51 @@
         backward(kept.at[r], cots.at[r], weights, normed.at[r], hidden.at[r], pre_grad.at[r], None, None)
 
     def ahead_second(i):
-        @pl.when(not_first)
-        def _():
-            relay_f[i].wait_recv()
-
-        @pl.when(s == 0)
-        def _():
-            edge_in[i].wait()
-
         forward(x2.at[half[i]], out2.at[half[i]], weights, fwd_normed, fwd_hidden)
+
+    def finish_mirrored():
+        ahead_second(1)
+        if staged:
+            pl.when(outer)(lambda: pl.semaphore_wait(turn, 1))
+        m_out.start()
 
     local[1].wait()
     local[2].wait()
     back_first(0)
-    local[3].wait()
-    ahead_first(0)
+    if staged:
+
+        pl.when(helper)(m_kept2.start)
+
+        @pl.when(helper)
+        def _():
+            k_via.wait_recv()
+            k_pass.start()
+    else:
+        m_kept2.start()
     m_cot.wait_recv()
     m_kept.wait_recv()
     back_first(1)
-    m_kept2.start()
-    m_x.wait_recv()
-    ahead_first(1)
+    even = lax.rem(s, 2) == 0
+    early = even & (s >= sections // 2)
+    soon = even & (s != sections // 2 - 2)
+    if staged:
+        pl.when(outer)(m_kept2.start)
+
+        @pl.when(inner)
+        def _():
+            m_x.start()
+
+        @pl.when(inner & (above > 0))
+        def _():
+            x_via.wait_recv()
+            x_pass.start()
+    else:
+        pl.when(not_first)(m_x.start)
+    local[3].wait()
+    ahead_first(0, soon)
     local[4].wait()
     back_second(0)
-    ahead_second(0)
-    out_own = pltpu.make_async_copy(out2.at[low], out_hbm.at[0, 0], lsem.at[9])
-    out_own.start()
-    ahead_second(1)
-    m_out.start()
+    ahead_first(1, early)
     m_kept2.wait_recv()
     back_second(1)
 
@@ -304,6 +344,15 @@
             sum_copy(i, peers[t - 1]).start()
 
         loop(per, pass_on)
+
+    @pl.when(s == 0)
+    def _():
+        for copy in edge_in:
+            copy.wait()
+        finish_mirrored()
+
+    ahead_first(1, jnp.logical_not(early))
+    ahead_first(0, jnp.logical_not(soon))
     loop(per, lambda q: give(g, q, q))
 
     def finish(q):
@@ -317,6 +366,24 @@
         total[rows] = total[rows] + part_recv[q].astype(F32)
 
     loop(per, finish)
+
+    if staged:
+
+        @pl.when(inner)
+        def _():
+            m_x.wait_send()
+            pl.when(above > 0)(x_pass.wait_send)
+            pl.semaphore_signal(turn, inc=1, device_id=(above, d), device_id_type=MESH)
+
+    @pl.when(not_first)
+    def _():
+        relay_f[1].wait_recv()
+        finish_mirrored()
+        relay_f[0].wait_recv()
+
+    ahead_second(0)
+    out_own = pltpu.make_async_copy(out2.at[low], out_hbm.at[0, 0], lsem.at[9])
+    out_own.start()
 
     def collect(q):
         rows = pl.ds(pl.multiple_of(q * CHUNK, CHUNK), CHUNK)
@@ -333,8 +400,14 @@
 
     out_own.wait()
     m_out.wait_recv()
-    for copy in (m_cot, m_kept, m_x, m_kept2, m_out):
+    for copy in (m_cot, m_kept, m_out):
         copy.wait_send()
+    if staged:
+        for here, copy in ((direct, m_kept2), (middle, k_via), (outer & not_first, x_via), (helper, k_pass)):
+            pl.when(here)(copy.wait_send)
+    else:
+        m_kept2.wait_send()
+        pl.when(not_first)(m_x.wait_send)
     for row in w_out + [p_own] + p_fwd:
         for copy in row:
             copy.wait_send()
@@ -386,6 +459,8 @@
             v((span, features), BF),
             v((span, width), BF),
             v((span, features), F32),
+            v((span, features), BF),
+            v((span, features), BF),
             v((pairs, CHUNK, columns), BF),
             v((pairs, CHUNK, columns), BF),
             v((CHUNK, columns), F32),
@@ -405,6 +480,9 @@
             dma((pairs,)),
             dma((sums,)),
             dma((sums,)),
+            dma((4,)),
+            dma((2,)),
+            pltpu.SemaphoreType.REGULAR,
         ],
         compiler_params=pltpu.CompilerParams(
             collective_id=0, has_side_effects=True, vmem_limit_bytes=60 * 2**20

time: 190 us -> 156 us (0.82)
  the two profiles are of different devices: /device:TPU:18 before, /device:TPU:28 now
where the time goes in v2:
time: 156 us
  Pallas kernels  149 us (96%)
  local copies, waits for them, and re-layouts  6.06 us (4%)
    pallas_call x1, Pallas kernels, on_device(): pl.pallas_call(functools.partial(kernel, sections, replicas), out_shape=(...  149 us
    unnamed x2, local copies, waits for them, and re-layouts  6.06 us

profile of v2, /device:TPU:28, one launch (start us, length us, event | category | flops | bytes accessed | tf_op | source)
XLA Modules:
  0.0 156.1 jit_solution(839496174507913908)
XLA Ops:
  0.6 149.4 %shard_map.77 = (bf16[2,1,128,2048]{3,2,1,0:T(8,128)(2,1)}, f32[1,512,1536]{2,1,0:T(8,128)}) custom-call(bf16[2,1,128,2048]{3,2,1,0:T(8,128)(2,1)} %x_hbm.1, bf16[2,1,128,2048]{3,2,1,0:T(8,128)(2,1)} %inc_hbm.1, bf16[2,1,128,2048]{3,2,1,0:T(8,128)(2,1)} %cot_hbm.1, bf16[2,1,128,2048]{3,2,1,0:T(8,128)(2,1)} %obj_hbm.1, ...), custom_call_target="tpu_custom_call" | custom-call | tf_op jit(solution)/shard_map/pallas_call | solution.py:439
  150.1 2.3 %copy.10 = bf16[2,1,128,2048]{3,2,1,0:T(8,128)(2,1)} copy(bf16[2,1,128,2048]{3,2,1,0:T(8,128)(2,1)} %get-tuple-element.4) | data formatting | bytes 2097152
  152.4 3.8 %copy.11 = f32[1,512,1536]{2,1,0:T(8,128)} copy(f32[1,512,1536]{2,1,0:T(8,128)} %get-tuple-element.5) | data formatting | bytes 6291456

commit v3 on v2

--- a/solution.py
+++ b/solution.py
@@ -94,7 +94,7 @@
     weights, x1, x2, kept, cots, normed, pre_grad, hidden, fo, fb, out2,
     fwd_normed, fwd_hidden, scratch, via_kept, via_x,
     part_send, part_recv, keep, sum_send, sum_recv, total,
-    lsem, wsem_s, wsem_r, psem_s, psem_r, msem_s, msem_r, rsem_s, rsem_r, gsem_s, gsem_r, ysem_s, ysem_r, vsem_s, vsem_r, turn,
+    lsem, wsem_s, wsem_r, psem_s, psem_r, msem_s, msem_r, rsem_s, rsem_r, gsem_s, gsem_r, ysem_s, ysem_r, vsem_s, vsem_r, turn, clear,
 ):
     s = lax.axis_index("section")
     d = lax.axis_index("dp")
@@ -224,9 +224,8 @@
         r = half[i]
         backward(kept.at[r], cots.at[r], weights, normed.at[r], hidden.at[r], pre_grad.at[r], fb.at[r], scratch)
 
-        @pl.when(not_first)
-        def _():
-            relay_b[i].start()
+    def send_back(i, here):
+        pl.when(here & not_first)(relay_b[i].start)
 
     def ahead_first(i, here):
         @pl.when(here & not_last)
@@ -256,11 +255,13 @@
         ahead_second(1)
         if staged:
             pl.when(outer)(lambda: pl.semaphore_wait(turn, 1))
+        pl.when(not_last)(lambda: pl.semaphore_wait(clear, 1))
         m_out.start()
 
     local[1].wait()
     local[2].wait()
     back_first(0)
+    send_back(0, inner if staged else True)
     if staged:
 
         pl.when(helper)(m_kept2.start)
@@ -276,9 +277,11 @@
     back_first(1)
     even = lax.rem(s, 2) == 0
     early = even & (s >= sections // 2)
-    soon = even & (s != sections // 2 - 2)
-    if staged:
+    if staged:
+        send_back(0, outer)
         pl.when(outer)(m_kept2.start)
+    send_back(1, True)
+    if staged:
 
         @pl.when(inner)
         def _():
@@ -291,7 +294,7 @@
     else:
         pl.when(not_first)(m_x.start)
     local[3].wait()
-    ahead_first(0, soon)
+    ahead_first(0, even)
     local[4].wait()
     back_second(0)
     ahead_first(1, early)
@@ -351,8 +354,18 @@
             copy.wait()
         finish_mirrored()
 
+    own_first = jnp.logical_not(even | middle) if staged else False
+    ahead_first(0, own_first)
     ahead_first(1, jnp.logical_not(early))
-    ahead_first(0, jnp.logical_not(soon))
+    ahead_first(0, jnp.logical_not(even | own_first))
+    if staged:
+
+        @pl.when(inner)
+        def _():
+            m_x.wait_send()
+            pl.when(above > 0)(x_pass.wait_send)
+            pl.semaphore_signal(turn, inc=1, device_id=(above, d), device_id_type=MESH)
+
     loop(per, lambda q: give(g, q, q))
 
     def finish(q):
@@ -367,17 +380,10 @@
 
     loop(per, finish)
 
-    if staged:
-
-        @pl.when(inner)
-        def _():
-            m_x.wait_send()
-            pl.when(above > 0)(x_pass.wait_send)
-            pl.semaphore_signal(turn, inc=1, device_id=(above, d), device_id_type=MESH)
-
     @pl.when(not_first)
     def _():
         relay_f[1].wait_recv()
+        pl.semaphore_signal(clear, inc=1, device_id=mirror, device_id_type=MESH)
         finish_mirrored()
         relay_f[0].wait_recv()
 
@@ -483,6 +489,7 @@
             dma((4,)),
             dma((2,)),
             pltpu.SemaphoreType.REGULAR,
+            pltpu.SemaphoreType.REGULAR,
         ],
         compiler_params=pltpu.CompilerParams(
             collective_id=0, has_side_effects=True, vmem_limit_bytes=60 * 2**20

time: 156 us -> 151 us (0.968)
  the two profiles are of different devices: /device:TPU:28 before, /device:TPU:6 now
where the time goes in v3:
time: 151 us; the launch traced here: 148 us
  Pallas kernels  141 us (93%)
  local copies, waits for them, and re-layouts  6.06 us (4%)
    pallas_call x1, Pallas kernels, on_device(): pl.pallas_call(functools.partial(kernel, sections, replicas), out_shape=(...  141 us
    unnamed x2, local copies, waits for them, and re-layouts  6.06 us

profile of v3, /device:TPU:6, one launch (start us, length us, event | category | flops | bytes accessed | tf_op | source)
XLA Modules:
  0.0 147.9 jit_solution(3775720379761978354)
XLA Ops:
  0.6 141.2 %shard_map.77 = (bf16[2,1,128,2048]{3,2,1,0:T(8,128)(2,1)}, f32[1,512,1536]{2,1,0:T(8,128)}) custom-call(bf16[2,1,128,2048]{3,2,1,0:T(8,128)(2,1)} %x_hbm.1, bf16[2,1,128,2048]{3,2,1,0:T(8,128)(2,1)} %inc_hbm.1, bf16[2,1,128,2048]{3,2,1,0:T(8,128)(2,1)} %cot_hbm.1, bf16[2,1,128,2048]{3,2,1,0:T(8,128)(2,1)} %obj_hbm.1, ...), custom_call_target="tpu_custom_call" | custom-call | tf_op jit(solution)/shard_map/pallas_call | solution.py:445
  141.8 2.3 %copy.10 = bf16[2,1,128,2048]{3,2,1,0:T(8,128)(2,1)} copy(bf16[2,1,128,2048]{3,2,1,0:T(8,128)(2,1)} %get-tuple-element.4) | data formatting | bytes 2097152
  144.1 3.8 %copy.11 = f32[1,512,1536]{2,1,0:T(8,128)} copy(f32[1,512,1536]{2,1,0:T(8,128)} %get-tuple-element.5) | data formatting | bytes 6291456

commit v4 on v3

--- a/solution.py
+++ b/solution.py
@@ -277,6 +277,7 @@
     back_first(1)
     even = lax.rem(s, 2) == 0
     early = even & (s >= sections // 2)
+    crossing = jnp.logical_not(even) & middle if staged else False
     if staged:
         send_back(0, outer)
         pl.when(outer)(m_kept2.start)
@@ -297,6 +298,8 @@
     ahead_first(0, even)
     local[4].wait()
     back_second(0)
+    if staged:
+        ahead_first(0, crossing)
     ahead_first(1, early)
     m_kept2.wait_recv()
     back_second(1)
@@ -354,10 +357,8 @@
             copy.wait()
         finish_mirrored()
 
-    own_first = jnp.logical_not(even | middle) if staged else False
-    ahead_first(0, own_first)
+    ahead_first(0, jnp.logical_not(even | crossing))
     ahead_first(1, jnp.logical_not(early))
-    ahead_first(0, jnp.logical_not(even | own_first))
     if staged:
 
         @pl.when(inner)
@@ -442,7 +443,7 @@
     dma = pltpu.SemaphoreType.DMA
     v = pltpu.VMEM
     any_space = pl.BlockSpec(memory_space=pl.ANY)
-    return pl.pallas_call(
+    results = pl.pallas_call(
         functools.partial(kernel, sections, replicas),
         out_shape=(
             jax.ShapeDtypeStruct(x.shape, BF),
@@ -495,6 +496,43 @@
             collective_id=0, has_side_effects=True, vmem_limit_bytes=60 * 2**20
         ),
     )(x, inc, cot, obj, kept, w)
+    return hand_out(*results)
+
+
+def hand_out(out, grads):
+    steps = 4
+    rows = grads.shape[1] // steps
+    count = steps + out.shape[0]
+
+    def body(out_ref, grads_ref, out_to, grads_to, out_mid, grads_mid, sem_in, sem_out):
+        parts = [(grads_ref, grads_mid, grads_to, (0, pl.ds(i * rows, rows))) for i in range(steps)]
+        parts += [(out_ref, out_mid, out_to, (i,)) for i in range(out.shape[0])]
+        taken = [pltpu.make_async_copy(a.at[at], b.at[at], sem_in.at[i]) for i, (a, b, _, at) in enumerate(parts)]
+        given = [pltpu.make_async_copy(b.at[at], c.at[at], sem_out.at[i]) for i, (_, b, c, at) in enumerate(parts)]
+        for copy in taken:
+            copy.start()
+        for one, two in zip(taken, given):
+            one.wait()
+            two.start()
+        for copy in given:
+            copy.wait()
+
+    any_space = pl.BlockSpec(memory_space=pl.ANY)
+    return pl.pallas_call(
+        body,
+        out_shape=(
+            jax.ShapeDtypeStruct(out.shape, out.dtype),
+            jax.ShapeDtypeStruct(grads.shape, grads.dtype),
+        ),
+        in_specs=[any_space] * 2,
+        out_specs=(any_space, any_space),
+        scratch_shapes=[
+            pltpu.VMEM(out.shape, out.dtype),
+            pltpu.VMEM(grads.shape, grads.dtype),
+            pltpu.SemaphoreType.DMA((count,)),
+            pltpu.SemaphoreType.DMA((count,)),
+        ],
+    )(out, grads)
 
 
 def solution(mesh):

time: 151 us -> 145 us (0.960); the launches traced: 148 us -> 145 us
  local copies, waits for them, and re-layouts: 6.06 us -> 0 us
  Pallas kernels: 141 us -> 144 us
    unnamed x2 -> x0, local copies, waits for them, and re-layouts: 6.06 us -> none
    pallas_call x0 -> x1, Pallas kernels: none -> 3.33 us  [hand_out(): pl.pallas_call(body, out_shape=(jax.ShapeDtypeStruct(out.shape, out.dtype...]
where the time goes in v4:
time: 145 us
  Pallas kernels  144 us (99%)
    pallas_call x1, Pallas kernels, on_device(): pl.pallas_call(functools.partial(kernel, sections, replicas), out_shape=(...  141 us
    pallas_call x1, Pallas kernels, hand_out(): pl.pallas_call(body, out_shape=(jax.ShapeDtypeStruct(out.shape, out.dtype...  3.33 us

profile of v4, /device:TPU:6, one launch (start us, length us, event | category | flops | bytes accessed | tf_op | source)
XLA Modules:
  0.0 145.1 jit_solution(1113240735596972826)
XLA Ops:
  0.6 141.2 %shard_map.77 = (bf16[2,1,128,2048]{3,2,1,0:T(8,128)(2,1)}, f32[1,512,1536]{2,1,0:T(8,128)}) custom-call(bf16[2,1,128,2048]{3,2,1,0:T(8,128)(2,1)} %x_hbm.1, bf16[2,1,128,2048]{3,2,1,0:T(8,128)(2,1)} %inc_hbm.1, bf16[2,1,128,2048]{3,2,1,0:T(8,128)(2,1)} %cot_hbm.1, bf16[2,1,128,2048]{3,2,1,0:T(8,128)(2,1)} %obj_hbm.1, ...), custom_call_target="tpu_custom_call" | custom-call | tf_op jit(solution)/shard_map/pallas_call | solution.py:446
  141.8 3.3 %shard_map.78 = (bf16[2,1,128,2048]{3,2,1,0:T(8,128)(2,1)}, f32[1,512,1536]{2,1,0:T(8,128)}) custom-call(bf16[2,1,128,2048]{3,2,1,0:T(8,128)(2,1)} %get-tuple-element.4.out_ref, f32[1,512,1536]{2,1,0:T(8,128)} %get-tuple-element.5.grads_ref), custom_call_target="tpu_custom_call" | custom-call | tf_op jit(solution)/shard_map/pallas_call | solution.py:521

commit v5 on v4

--- a/solution.py
+++ b/solution.py
@@ -500,7 +500,7 @@
 
 
 def hand_out(out, grads):
-    steps = 4
+    steps = 8
     rows = grads.shape[1] // steps
     count = steps + out.shape[0]
 

time: 145 us -> 146 us (level)
  no operation moved by 1% of the time
where the time goes in v5:
time: 146 us
  Pallas kernels  145 us (99%)
    pallas_call x1, Pallas kernels, on_device(): pl.pallas_call(functools.partial(kernel, sections, replicas), out_shape=(...  141 us
    pallas_call x1, Pallas kernels, hand_out(): pl.pallas_call(body, out_shape=(jax.ShapeDtypeStruct(out.shape, out.dtype...  3.73 us

profile of v5, /device:TPU:6, one launch (start us, length us, event | category | flops | bytes accessed | tf_op | source)
XLA Modules:
  0.0 145.5 jit_solution(3965513937194996941)
XLA Ops:
  0.6 141.2 %shard_map.77 = (bf16[2,1,128,2048]{3,2,1,0:T(8,128)(2,1)}, f32[1,512,1536]{2,1,0:T(8,128)}) custom-call(bf16[2,1,128,2048]{3,2,1,0:T(8,128)(2,1)} %x_hbm.1, bf16[2,1,128,2048]{3,2,1,0:T(8,128)(2,1)} %inc_hbm.1, bf16[2,1,128,2048]{3,2,1,0:T(8,128)(2,1)} %cot_hbm.1, bf16[2,1,128,2048]{3,2,1,0:T(8,128)(2,1)} %obj_hbm.1, ...), custom_call_target="tpu_custom_call" | custom-call | tf_op jit(solution)/shard_map/pallas_call | solution.py:446
  141.8 3.7 %shard_map.78 = (bf16[2,1,128,2048]{3,2,1,0:T(8,128)(2,1)}, f32[1,512,1536]{2,1,0:T(8,128)}) custom-call(bf16[2,1,128,2048]{3,2,1,0:T(8,128)(2,1)} %get-tuple-element.4.out_ref, f32[1,512,1536]{2,1,0:T(8,128)} %get-tuple-element.5.grads_ref), custom_call_target="tpu_custom_call" | custom-call | tf_op jit(solution)/shard_map/pallas_call | solution.py:521
